TPU v7x, 512 devices: a whole 4x8x8 slice. The times are simulated.
512 devices in a mesh: dp: 64 (over z, x, core), class: 8 (over y).
Axes of the slice: x: 4, y: 8, z: 8, core: 2. Of those that a mesh axis runs over, the one named last changes fastest.
Arguments:
- embeddings: bfloat16 [16384, 1024], P('dp', 'class'), may hold values from -28 to 28, as said below
- labels: bfloat16 [16384, 4096], P('dp', 'class'), may hold values from -55 to 55
- head_weight: bfloat16 [1024, 4096], P(None, 'class'), may hold values from -0.1875 to 0.1875
- send_blocks: int32 [64, 64], P('dp'), may hold values from 0 to 1
- nbr_source: int32 [16384, 32], P('dp'), may hold values from 0 to 63
- nbr_offset: int32 [16384, 32], P('dp'), may hold values from 0 to 127
- counts: int32 [16384], P('dp'), may hold values from 1 to 32
Outputs:
- target_logits: bfloat16 [16384, 4096], P('dp', 'class')
- head_grad: bfloat16 [1024, 4096], P(None, 'class')
Inputs may be any that keep to these rules, and one draw needn't show every extreme that they name: Each image of the embeddings has entries within the range. `send_blocks`: entry [p, q] names which of dp index p's own 2 blocks dp index q receives from p. The neighbour lies in the block that this dp index receives from dp index nbr_source. Only the first counts[r] neighbours of image r are used.
All inputs are finite; a program needn't handle non-finite values.
Results may differ from a plain program's by a relative error of at most 0.0062.
Values may be sent and summed in bfloat16 or wider, within the bound.
A program may use at most 64 MiB of HBM per device.

v0:
```python
import math
import jax
import jax.numpy as jnp
from jax import lax
from jax.sharding import PartitionSpec as P

D = 1024
C = 4096
BLOCK = 128


def _combine_stats(local_max, local_sum):
    both = lax.all_gather(jnp.stack([local_max, local_sum], axis=0), "class", axis=0)
    maxes, sums = (both[:, 0], both[:, 1])
    top = jnp.max(maxes, axis=0)
    total = jnp.sum(sums * jnp.exp(maxes - top[None, :]), axis=0)
    return (top, total)


def on_device(embeddings, labels, head_weight, send_blocks, nbr_source, nbr_offset, counts):
    rows = embeddings.shape[0]
    width_part = embeddings.shape[1]
    class_part = labels.shape[1]
    dp_count = lax.axis_size("dp")
    nbrs = nbr_source.shape[1]
    picks = send_blocks[0]
    out_emb = embeddings.reshape(rows // BLOCK, BLOCK, width_part)[picks]
    out_lab = labels.reshape(rows // BLOCK, BLOCK, class_part)[picks]
    pool_emb = lax.all_to_all(out_emb, "dp", split_axis=0, concat_axis=0, tiled=True)
    pool_lab = lax.all_to_all(out_lab, "dp", split_axis=0, concat_axis=0, tiled=True)
    pool_rows = dp_count * BLOCK
    pool_emb = pool_emb.reshape(pool_rows, width_part)
    pool_lab = pool_lab.reshape(pool_rows, class_part)
    located = nbr_source * BLOCK + nbr_offset
    full_emb = lax.all_gather(embeddings, "class", axis=1, tiled=True)
    head = jnp.dot(full_emb, head_weight, preferred_element_type=jnp.float32)
    h_top, h_total = _combine_stats(
        jnp.max(head, axis=1), jnp.sum(jnp.exp(head - jnp.max(head, axis=1, keepdims=True)), axis=1)
    )
    prob_head = jnp.exp(head - h_top[:, None]) / h_total[:, None]
    near = pool_emb[located]
    partial_value = jnp.einsum("rd,rkd->rk", embeddings, near, preferred_element_type=jnp.float32)
    scores = lax.psum(partial_value, "class")
    valid = lax.broadcasted_iota(jnp.int32, (rows, nbrs), 1) < counts[:, None]
    logits = jnp.where(valid, scores / math.sqrt(D), -1e30)
    top = jnp.max(logits, axis=1, keepdims=True)
    expd = jnp.where(valid, jnp.exp(logits - top), 0.0)
    weights = (expd / jnp.sum(expd, axis=1, keepdims=True)).astype(jnp.bfloat16)
    row_ids = lax.broadcasted_iota(jnp.int32, (rows, nbrs), 0)
    dense = (
        jnp.zeros((rows, pool_rows), jnp.float32)
        .at[row_ids, located]
        .add(weights.astype(jnp.float32))
    )
    dense_hi = dense.astype(jnp.bfloat16)
    dense_lo = (dense - dense_hi.astype(jnp.float32)).astype(jnp.bfloat16)
    spread = jnp.dot(dense_hi, pool_lab, preferred_element_type=jnp.float32) + jnp.dot(
        dense_lo, pool_lab, preferred_element_type=jnp.float32
    )
    target = 4.0 * spread + labels.astype(jnp.float32)
    z_local = jnp.max(target, axis=1)
    z_top, z_total = _combine_stats(z_local, jnp.sum(jnp.exp(target - z_local[:, None]), axis=1))
    prob_target = jnp.exp(target - z_top[:, None]) / z_total[:, None]
    diff = (C * (prob_head - prob_target)).astype(jnp.bfloat16)
    part_grad = lax.dot_general(
        full_emb, diff, (((0,), (0,)), ((), ())), preferred_element_type=jnp.float32
    )
    scale = 1.0 / math.sqrt(rows * dp_count)
    limit = 0.5 * math.sqrt(D * C)
    summed = lax.psum_scatter(part_grad, "dp", scatter_dimension=0, tiled=True) * scale
    squared = lax.psum(jnp.sum(summed * summed), ("dp", "class"))
    factor = jnp.minimum(1.0, limit / jnp.sqrt(squared))
    head_grad = lax.all_gather((summed * factor).astype(jnp.bfloat16), "dp", axis=0, tiled=True)
    return (target.astype(jnp.bfloat16), head_grad)


def solution(mesh):
    return jax.shard_map(
        on_device,
        mesh=mesh,
        in_specs=(
            P("dp", "class"),
            P("dp", "class"),
            P(None, "class"),
            P("dp", None),
            P("dp", None),
            P("dp", None),
            P("dp"),
        ),
        out_specs=(P("dp", "class"), P(None, "class")),
        check_vma=False,
    )
```

profile of v0, /device:TPU:1, one launch (start us, length us, event | category | flops | bytes accessed | tf_op | source)
XLA Modules:
  0.0 644.6 jit_solution(2418893639809104688)
XLA Ops:
  8.0 3.0 gather_fusion
  11.0 14.8 %all-to-all-start = ((bf16[64,128,128]{2,1,0:T(8,128)(2,1)}), bf16[64,128,128]{2,1,0:T(8,128)(2,1)S(1)}, u32[]{:S(2)}, u32[]{:S(2)}) async-start(bf16[64,128,128]{2,1,0:T(8,128)(2,1)} %gather_fusion), calls=%async_computation | async-start | bytes 4194304 | tf_op jit(solution)/shard_map/all_to_all | solution.py:29
  25.8 5.4 gather_fusion.2
  31.2 44.3 %all-to-all-done = bf16[64,128,128]{2,1,0:T(8,128)(2,1)S(1)} async-done(((bf16[64,128,128]{2,1,0:T(8,128)(2,1)}), bf16[64,128,128]{2,1,0:T(8,128)(2,1)S(1)}, u32[]{:S(2)}, u32[]{:S(2)}) %all-to-all-start) | async-done | bytes 2097184 | tf_op jit(solution)/shard_map/all_to_all | solution.py:29
  75.5 7.2 %all-to-all-start.1 = ((bf16[64,128,512]{2,1,0:T(8,128)(2,1)}), bf16[64,128,512]{2,1,0:T(8,128)(2,1)}, u32[]{:S(2)}, u32[]{:S(2)}) async-start(bf16[64,128,512]{2,1,0:T(8,128)(2,1)} %gather_fusion.2), calls=%async_computation.1 | async-start | bytes 16777216 | tf_op jit(solution)/shard_map/all_to_all | solution.py:30
  85.3 1.6 reshape.99
  86.9 1.0 reshape.85
  87.9 22.7 %all_gather.18 = bf16[256,1024]{1,0:T(8,128)(2,1)S(1)} all-gather(bf16[256,128]{1,0:T(8,128)(2,1)S(1)} %copy-done.2), channel_id=1, replica_groups=mesh['dp'=64,'class'=8] {'class'}, dimensions={1}, use_global_device_ids=true | all-gather | bytes 589824 | tf_op jit(solution)/shard_map/all_gather | solution.py:35
  112.9 18.0 %all-gather.2 = f32[8,2,256]{2,1,0:T(2,128)S(1)} all-gather(f32[1,2,256]{2,1,0:T(2,128)S(1)} %maximum_bitcast_fusion), channel_id=2, replica_groups=mesh['dp'=64,'class'=8] {'class'}, dimensions={0}, use_global_device_ids=true | all-gather | bytes 18432 | tf_op jit(solution)/shard_map/all_gather | solution.py:13
  131.0 29.2 %gather_fusion.1 = bf16[8192,128]{1,0:T(8,128)(2,1)} fusion(bf16[8192,128]{1,0:T(8,128)(2,1)S(1)} %bitcast.55, s32[8192]{0:T(1024)S(1)} %broadcast_clamp_fusion), kind=kCustom, calls=%fused_computation.1 | custom fusion | bytes 4227072 | tf_op jit(solution)/shard_map/gather | solution.py:41
  160.2 2.8 fusion.20
  163.0 24.4 %psum.14 = f32[256,32]{1,0:T(8,128)S(1)} all-reduce(f32[256,32]{1,0:T(8,128)S(1)} %bitcast.61), channel_id=1, replica_groups=mesh['dp'=64,'class'=8] {'class'}, use_global_device_ids=true, to_apply=%region_0.0 | all-reduce | flops 8192 | bytes 65536 | tf_op jit(solution)/shard_map/psum | solution.py:43
  188.1 47.1 %scatter_custom_fusion = f32[2097152]{0:T(1024)} fusion(s32[8192]{0:T(1024)} %reshape.99, f32[8192]{0:T(1024)S(1)} %reshape.101, f32[]{:T(128)} %constant.13.clone.1), kind=kCustom, calls=%fused_computation.6 | custom fusion | flops 8192 | bytes 8389120
  235.2 9.4 %reshape.74 = f32[256,8192]{1,0:T(8,128)} reshape(f32[2097152]{0:T(1024)} %scatter_custom_fusion) | data formatting | bytes 16777216 | tf_op jit(solution)/shard_map/scatter-add | solution.py:53
  244.6 21.0 %all-to-all-done.1 = bf16[64,128,512]{2,1,0:T(8,128)(2,1)} async-done(((bf16[64,128,512]{2,1,0:T(8,128)(2,1)}), bf16[64,128,512]{2,1,0:T(8,128)(2,1)}, u32[]{:S(2)}, u32[]{:S(2)}) %all-to-all-start.1) | async-done | bytes 8388640 | tf_op jit(solution)/shard_map/all_to_all | solution.py:30
  265.6 10.6 %fusion = f32[256,512]{1,0:T(8,128)S(1)} fusion(bf16[8192,512]{1,0:T(8,128)(2,1)} %bitcast.10, f32[256,8192]{1,0:T(8,128)} %reshape.74), kind=kOutput, calls=%fused_computation.5 | convolution fusion | flops 2155872256 | bytes 17301504 | tf_op jit(solution)/shard_map/dot_general | solution.py:57
  276.3 5.9 fusion.33
  283.1 18.3 %all-gather.3 = f32[8,2,256]{2,1,0:T(2,128)S(1)} all-gather(f32[1,2,256]{2,1,0:T(2,128)S(1)} %maximum_bitcast_fusion.1), channel_id=3, replica_groups=mesh['dp'=64,'class'=8] {'class'}, dimensions={0}, use_global_device_ids=true | all-gather | bytes 18432 | tf_op jit(solution)/shard_map/all_gather | solution.py:13
  302.1 1.9 copy.28
  304.1 147.5 %reduce-scatter.4.cloned.1.call-done = f32[16,512]{1,0:T(8,128)} async-done(((f32[1024,512]{1,0:T(8,128)}), f32[16,512]{1,0:T(8,128)}) %reduce-scatter.4.cloned.1.call-update) | async-done | bytes 32784 | tf_op jit(solution)/shard_map/reduce_scatter | solution.py:70
  453.2 100.5 %psum.15 = f32[]{:T(128)} all-reduce(f32[]{:T(128)} %multiply_reduce_fusion), channel_id=1, replica_groups=mesh['dp'=64,'class'=8] {'dp','class'}, use_global_device_ids=true, to_apply=%region_14.15 | all-reduce | flops 1 | bytes 8 | tf_op jit(solution)/shard_map/psum | solution.py:71
  554.3 1.4 multiply_convert_fusion.2
  555.7 79.7 %all-gather.6.cloned.1.call-done = bf16[1024,512]{1,0:T(8,128)(2,1)} async-done(((bf16[16,512]{1,0:T(8,128)(2,1)}), bf16[1024,512]{1,0:T(8,128)(2,1)}) %all-gather.6.cloned.1.call-update) | async-done | bytes 1048592 | tf_op jit(solution)/shard_map/all_gather | solution.py:73
  635.5 2.3 copy.49
  (54 shorter events, 9.7 us)
Async XLA Ops:
  7.2 104.2 %copy-start = (bf16[1024,512]{1,0:T(8,128)(2,1)S(1)}, bf16[1024,512]{1,0:T(8,128)(2,1)}, u32[]{:S(2)}) copy-start(bf16[1024,512]{1,0:T(8,128)(2,1)} %param.9) | copy-start | bytes 3145732
  7.2 18.6 %copy-start.1 = (bf16[256,512]{1,0:T(8,128)(2,1)S(1)}, bf16[256,512]{1,0:T(8,128)(2,1)}, u32[]{:S(2)}) copy-start(bf16[256,512]{1,0:T(8,128)(2,1)} %param.8) | copy-start | bytes 786436
  11.0 64.5 %all-to-all-start = ((bf16[64,128,128]{2,1,0:T(8,128)(2,1)}), bf16[64,128,128]{2,1,0:T(8,128)(2,1)S(1)}, u32[]{:S(2)}, u32[]{:S(2)}) async-start(bf16[64,128,128]{2,1,0:T(8,128)(2,1)} %gather_fusion), calls=%async_computation | async-start | bytes 4194304 | tf_op jit(solution)/shard_map/all_to_all | solution.py:29
  31.2 51.6 %copy-start.8 = (s32[256,32]{0,1:T(8,128)S(1)}, s32[256,32]{0,1:T(8,128)}, u32[]{:S(2)}) copy-start(s32[256,32]{0,1:T(8,128)} %param.12) | copy-start | bytes 98308
  31.2 53.2 %copy-start.10 = (s32[2]{0:T(128)S(1)}, s32[2]{0:T(128)}, u32[]{:S(2)}) copy-start(s32[2]{0:T(128)} %constant.33) | copy-start | bytes 28
  31.2 53.2 %copy-start.11 = (s32[2]{0:T(128)S(1)}, s32[2]{0:T(128)}, u32[]{:S(2)}) copy-start(s32[2]{0:T(128)} %constant.36) | copy-start | bytes 28
  31.2 56.7 %copy-start.2 = (bf16[256,128]{1,0:T(8,128)(2,1)S(1)}, bf16[256,128]{1,0:T(8,128)(2,1)}, u32[]{:S(2)}) copy-start(bf16[256,128]{1,0:T(8,128)(2,1)} %param.7) | copy-start | bytes 196612
  75.5 190.1 %all-to-all-start.1 = ((bf16[64,128,512]{2,1,0:T(8,128)(2,1)}), bf16[64,128,512]{2,1,0:T(8,128)(2,1)}, u32[]{:S(2)}, u32[]{:S(2)}) async-start(bf16[64,128,512]{2,1,0:T(8,128)(2,1)} %gather_fusion.2), calls=%async_computation.1 | async-start | bytes 16777216 | tf_op jit(solution)/shard_map/all_to_all | solution.py:30
  82.7 368.9 %reduce-scatter.4.cloned.1.call-start = ((), (), s32[]{:S(2)}) async-start(), calls=%async_computation.4 | async-start | bytes 2129920 | tf_op jit(solution)/shard_map/reduce_scatter | solution.py:70
  110.6 0.8 copy-start.4
  111.9 0.8 copy-start.6
  131.0 56.4 %copy-start.9 = (s32[256]{0:T(256)S(1)}, s32[256]{0:T(256)}, u32[]{:S(2)}) copy-start(s32[256]{0:T(256)} %param.13) | copy-start | bytes 3076
  265.6 10.6 %copy-start.3 = (f32[256,8192]{1,0:T(8,128)S(1)}, f32[256,8192]{1,0:T(8,128)}, u32[]{:S(2)}) copy-start(f32[256,8192]{1,0:T(8,128)} %reshape.74) | copy-start | bytes 25165828
  276.3 25.1 %copy-start.5 = (bf16[256,1024]{1,0:T(8,128)(2,1)S(1)}, bf16[256,1024]{1,0:T(8,128)(2,1)}, u32[]{:S(2)}) copy-start(bf16[256,1024]{1,0:T(8,128)(2,1)} %copy-done.4) | copy-start | bytes 1572868
  276.3 25.1 %copy-start.7 = (f32[256,512]{1,0:T(8,128)S(1)}, f32[256,512]{1,0:T(8,128)}, u32[]{:S(2)}) copy-start(f32[256,512]{1,0:T(8,128)} %copy-done.6) | copy-start | bytes 1572868
  304.0 331.4 %all-gather.6.cloned.1.call-start = ((), (), s32[]{:S(2)}) async-start(), calls=%async_computation.3 | async-start | bytes 1064960 | tf_op jit(solution)/shard_map/all_gather | solution.py:73
Sparse Core Ops, SparseCore 0:
  304.2 147.3 reduce-scatter.3
  555.8 79.5 all-gather.5
where the time goes:
time: 645 us
  waiting for transfers between devices  293 us (45%)
  blocking collectives  184 us (29%)
  local copies, waits for them, and re-layouts  57.8 us (9%)
  other arithmetic  52.6 us (8%)
  starting transfers between devices  22.2 us (3%)
  matrix products  20.5 us (3%)
  between operations  15 us (2%)
    reduce_scatter x1, waiting for transfers between devices, on_device(): lax.psum_scatter(part_grad, 'dp', scatter_dimension=0, tiled=True) * scale  148 us
    psum x1, blocking collectives, on_device(): squared = lax.psum(jnp.sum(summed * summed), ('dp', 'class'))  100 us
    all_gather x1, waiting for transfers between devices, on_device(): lax.all_gather((summed * factor).astype(jnp.bfloat16), 'dp', axis=0, tile...  79.7 us
    unnamed x6, other arithmetic  47.3 us
    all_to_all x1, waiting for transfers between devices, on_device(): lax.all_to_all(out_emb, 'dp', split_axis=0, concat_axis=0, tiled=True)  44.3 us
    all_gather x2, blocking collectives, _combine_stats(): lax.all_gather(jnp.stack([local_max, local_sum], axis=0), 'class', axis=0)  36.2 us
    gather x1, local copies, waits for them, and re-layouts, on_device(): near = pool_emb[located]  29.2 us
    psum x1, blocking collectives, on_device(): scores = lax.psum(partial_value, 'class')  24.4 us
  transfers between devices with their start and end apart: 4, of which 4 were waited for; matrix products, arithmetic and copies ran while one was open for 16% of the time, Pallas kernels for 0%

commit v1 on v0

--- a/solution.py
+++ b/solution.py
@@ -1,3 +1,4 @@
+import functools
 import math
 import jax
 import jax.numpy as jnp
@@ -7,6 +8,16 @@
 D = 1024
 C = 4096
 BLOCK = 128
+
+
+def cut_the_spans(m, dim_i):
+    return jnp.concatenate(
+        lax.all_to_all(jnp.stack([m for _ in range(lax.psum(1, "class"))], axis=0), "class", 0, 0),
+        dim_i,
+    )
+
+
+_update_slabs = functools.partial(cut_the_spans, dim_i=1)
 
 
 def _combine_stats(local_max, local_sum):
@@ -32,7 +43,7 @@
     pool_emb = pool_emb.reshape(pool_rows, width_part)
     pool_lab = pool_lab.reshape(pool_rows, class_part)
     located = nbr_source * BLOCK + nbr_offset
-    full_emb = lax.all_gather(embeddings, "class", axis=1, tiled=True)
+    full_emb = _update_slabs(embeddings)
     head = jnp.dot(full_emb, head_weight, preferred_element_type=jnp.float32)
     h_top, h_total = _combine_stats(
         jnp.max(head, axis=1), jnp.sum(jnp.exp(head - jnp.max(head, axis=1, keepdims=True)), axis=1)

time: 645 us -> 667 us (1.034)
  waiting for transfers between devices: 293 us -> 328 us
  blocking collectives: 184 us -> 159 us
  starting transfers between devices: 22.2 us -> 32 us
    all_to_all x1, waiting for transfers between devices: 21 us -> 45 us  [on_device(): lax.all_to_all(out_lab, 'dp', split_axis=0, concat_axis=0, tiled=True)]
    all_gather x1 -> x0, blocking collectives: 22.7 us -> none  [on_device(): full_emb = lax.all_gather(embeddings, 'class', axis=1, tiled=True)]
    all_to_all x0 -> x1, waiting for transfers between devices: none -> 11.1 us  [cut_the_spans(): lax.all_to_all(jnp.stack([m for _ in range(lax.psum(1, 'class'))], axis=0...]
    all_to_all x0 -> x1, starting transfers between devices: none -> 7.65 us  [cut_the_spans(): lax.all_to_all(jnp.stack([m for _ in range(lax.psum(1, 'class'))], axis=0...]
  transfers between devices with their start and end apart: 4 -> 5, of which waited for: 4 -> 5; matrix products, arithmetic and copies ran while one was open for 16% -> 16% of each run, Pallas kernels for 0% -> 0%
where the time goes in v1:
time: 667 us; the launch traced here: 666 us
  waiting for transfers between devices  328 us (49%)
  blocking collectives  159 us (24%)
  local copies, waits for them, and re-layouts  58.1 us (9%)
  other arithmetic  52.4 us (8%)
  starting transfers between devices  32 us (5%)
  matrix products  21.6 us (3%)
  between operations  15 us (2%)
    reduce_scatter x1, waiting for transfers between devices, on_device(): lax.psum_scatter(part_grad, 'dp', scatter_dimension=0, tiled=True) * scale  148 us
    psum x1, blocking collectives, on_device(): squared = lax.psum(jnp.sum(summed * summed), ('dp', 'class'))  101 us
    all_gather x1, waiting for transfers between devices, on_device(): lax.all_gather((summed * factor).astype(jnp.bfloat16), 'dp', axis=0, tile...  79.7 us
    unnamed x6, other arithmetic  47.9 us
    all_to_all x1, waiting for transfers between devices, on_device(): lax.all_to_all(out_lab, 'dp', split_axis=0, concat_axis=0, tiled=True)  45 us
    all_to_all x1, waiting for transfers between devices, on_device(): lax.all_to_all(out_emb, 'dp', split_axis=0, concat_axis=0, tiled=True)  44.3 us
    all_gather x2, blocking collectives, _combine_stats(): lax.all_gather(jnp.stack([local_max, local_sum], axis=0), 'class', axis=0)  33.5 us
    gather x1, local copies, waits for them, and re-layouts, on_device(): near = pool_emb[located]  29.2 us
  transfers between devices with their start and end apart: 5, of which 5 were waited for; matrix products, arithmetic and copies ran while one was open for 16% of the time, Pallas kernels for 0%

profile of v1, /device:TPU:1, one launch (start us, length us, event | category | flops | bytes accessed | tf_op | source)
XLA Modules:
  0.0 665.5 jit_solution(3290719772116988344)
XLA Ops:
  9.1 7.7 %all-to-all-start.2 = ((bf16[8,256,128]{1,2,0:T(8,128)(2,1)}), bf16[8,256,128]{1,2,0:T(8,128)(2,1)S(1)}, u32[]{:S(2)}, u32[]{:S(2)}) async-start(bf16[8,256,128]{1,2,0:T(8,128)(2,1)} %stack.14), calls=%async_computation.2 | async-start | bytes 1048576 | tf_op jit(solution)/shard_map/all_to_all | solution.py:15
  17.4 3.0 gather_fusion
  20.4 11.1 %all-to-all-done.2 = bf16[8,256,128]{1,2,0:T(8,128)(2,1)S(1)} async-done(((bf16[8,256,128]{1,2,0:T(8,128)(2,1)}), bf16[8,256,128]{1,2,0:T(8,128)(2,1)S(1)}, u32[]{:S(2)}, u32[]{:S(2)}) %all-to-all-start.2) | async-done | bytes 524320 | tf_op jit(solution)/shard_map/all_to_all | solution.py:15
  32.3 17.0 %all-to-all-start = ((bf16[64,128,128]{2,1,0:T(8,128)(2,1)}), bf16[64,128,128]{2,1,0:T(8,128)(2,1)S(1)}, u32[]{:S(2)}, u32[]{:S(2)}) async-start(bf16[64,128,128]{2,1,0:T(8,128)(2,1)} %gather_fusion), calls=%async_computation | async-start | bytes 4194304 | tf_op jit(solution)/shard_map/all_to_all | solution.py:40
  49.3 5.4 gather_fusion.2
  54.7 44.3 %all-to-all-done = bf16[64,128,128]{2,1,0:T(8,128)(2,1)S(1)} async-done(((bf16[64,128,128]{2,1,0:T(8,128)(2,1)}), bf16[64,128,128]{2,1,0:T(8,128)(2,1)S(1)}, u32[]{:S(2)}, u32[]{:S(2)}) %all-to-all-start) | async-done | bytes 2097184 | tf_op jit(solution)/shard_map/all_to_all | solution.py:40
  99.0 7.2 %all-to-all-start.1 = ((bf16[64,128,512]{2,1,0:T(8,128)(2,1)}), bf16[64,128,512]{2,1,0:T(8,128)(2,1)}, u32[]{:S(2)}, u32[]{:S(2)}) async-start(bf16[64,128,512]{2,1,0:T(8,128)(2,1)} %gather_fusion.2), calls=%async_computation.1 | async-start | bytes 16777216 | tf_op jit(solution)/shard_map/all_to_all | solution.py:41
  110.4 1.6 fusion.34
  112.2 18.0 %all-gather.2 = f32[8,2,256]{2,1,0:T(2,128)S(1)} all-gather(f32[1,2,256]{2,1,0:T(2,128)S(1)} %maximum_bitcast_fusion), channel_id=2, replica_groups=mesh['dp'=64,'class'=8] {'class'}, dimensions={0}, use_global_device_ids=true | all-gather | bytes 18432 | tf_op jit(solution)/shard_map/all_gather | solution.py:24
  130.3 29.2 %gather_fusion.1 = bf16[8192,128]{1,0:T(8,128)(2,1)} fusion(bf16[8192,128]{1,0:T(8,128)(2,1)S(1)} %bitcast.58, s32[8192]{0:T(1024)S(1)} %broadcast_clamp_fusion), kind=kCustom, calls=%fused_computation.1 | custom fusion | bytes 4227072 | tf_op jit(solution)/shard_map/gather | solution.py:52
  159.6 2.8 fusion.20
  162.3 24.6 %psum.14 = f32[256,32]{1,0:T(8,128)S(1)} all-reduce(f32[256,32]{1,0:T(8,128)S(1)} %bitcast.66), channel_id=1, replica_groups=mesh['dp'=64,'class'=8] {'class'}, use_global_device_ids=true, to_apply=%region_0.0 | all-reduce | flops 8192 | bytes 65536 | tf_op jit(solution)/shard_map/psum | solution.py:54
  187.6 47.1 %scatter_custom_fusion = f32[2097152]{0:T(1024)} fusion(s32[8192]{0:T(1024)} %reshape.109, f32[8192]{0:T(1024)S(1)} %reshape.111, f32[]{:T(128)} %constant.13.clone.1), kind=kCustom, calls=%fused_computation.6 | custom fusion | flops 8192 | bytes 8389120
  234.7 9.4 %reshape.84 = f32[256,8192]{1,0:T(8,128)} reshape(f32[2097152]{0:T(1024)} %scatter_custom_fusion) | data formatting | bytes 16777216 | tf_op jit(solution)/shard_map/scatter-add | solution.py:64
  244.1 45.0 %all-to-all-done.1 = bf16[64,128,512]{2,1,0:T(8,128)(2,1)} async-done(((bf16[64,128,512]{2,1,0:T(8,128)(2,1)}), bf16[64,128,512]{2,1,0:T(8,128)(2,1)}, u32[]{:S(2)}, u32[]{:S(2)}) %all-to-all-start.1) | async-done | bytes 8388640 | tf_op jit(solution)/shard_map/all_to_all | solution.py:41
  289.1 10.6 %fusion = f32[256,512]{1,0:T(8,128)S(1)} fusion(bf16[8192,512]{1,0:T(8,128)(2,1)} %bitcast.10, f32[256,8192]{1,0:T(8,128)} %reshape.84), kind=kOutput, calls=%fused_computation.5 | convolution fusion | flops 2155872256 | bytes 17301504 | tf_op jit(solution)/shard_map/dot_general | solution.py:68
  299.8 5.9 fusion.33
  306.5 15.4 %all-gather.3 = f32[8,2,256]{2,1,0:T(2,128)S(1)} all-gather(f32[1,2,256]{2,1,0:T(2,128)S(1)} %maximum_bitcast_fusion.1), channel_id=3, replica_groups=mesh['dp'=64,'class'=8] {'class'}, dimensions={0}, use_global_device_ids=true | all-gather | bytes 18432 | tf_op jit(solution)/shard_map/all_gather | solution.py:24
  322.8 1.9 copy.31
  324.8 147.8 %reduce-scatter.4.cloned.1.call-done = f32[16,512]{1,0:T(8,128)} async-done(((f32[1024,512]{1,0:T(8,128)}), f32[16,512]{1,0:T(8,128)}) %reduce-scatter.4.cloned.1.call-update) | async-done | bytes 32784 | tf_op jit(solution)/shard_map/reduce_scatter | solution.py:81
  474.1 100.5 %psum.15 = f32[]{:T(128)} all-reduce(f32[]{:T(128)} %multiply_reduce_fusion), channel_id=1, replica_groups=mesh['dp'=64,'class'=8] {'dp','class'}, use_global_device_ids=true, to_apply=%region_14.15 | all-reduce | flops 1 | bytes 8 | tf_op jit(solution)/shard_map/psum | solution.py:82
  575.3 1.4 multiply_convert_fusion.2
  576.7 79.7 %all-gather.6.cloned.1.call-done = bf16[1024,512]{1,0:T(8,128)(2,1)} async-done(((bf16[16,512]{1,0:T(8,128)(2,1)}), bf16[1024,512]{1,0:T(8,128)(2,1)}) %all-gather.6.cloned.1.call-update) | async-done | bytes 1048592 | tf_op jit(solution)/shard_map/all_gather | solution.py:84
  656.4 2.3 copy.52
  (59 shorter events, 11.8 us)
Async XLA Ops:
  7.2 103.3 %copy-start = (bf16[1024,512]{1,0:T(8,128)(2,1)S(1)}, bf16[1024,512]{1,0:T(8,128)(2,1)}, u32[]{:S(2)}) copy-start(bf16[1024,512]{1,0:T(8,128)(2,1)} %param.9) | copy-start | bytes 3145732
  7.2 42.1 %copy-start.1 = (bf16[256,512]{1,0:T(8,128)(2,1)S(1)}, bf16[256,512]{1,0:T(8,128)(2,1)}, u32[]{:S(2)}) copy-start(bf16[256,512]{1,0:T(8,128)(2,1)} %param.8) | copy-start | bytes 786436
  9.1 22.4 %all-to-all-start.2 = ((bf16[8,256,128]{1,2,0:T(8,128)(2,1)}), bf16[8,256,128]{1,2,0:T(8,128)(2,1)S(1)}, u32[]{:S(2)}, u32[]{:S(2)}) async-start(bf16[8,256,128]{1,2,0:T(8,128)(2,1)} %stack.14), calls=%async_computation.2 | async-start | bytes 1048576 | tf_op jit(solution)/shard_map/all_to_all | solution.py:15
  31.5 0.8 copy-start.4
  32.3 66.7 %all-to-all-start = ((bf16[64,128,128]{2,1,0:T(8,128)(2,1)}), bf16[64,128,128]{2,1,0:T(8,128)(2,1)S(1)}, u32[]{:S(2)}, u32[]{:S(2)}) async-start(bf16[64,128,128]{2,1,0:T(8,128)(2,1)} %gather_fusion), calls=%async_computation | async-start | bytes 4194304 | tf_op jit(solution)/shard_map/all_to_all | solution.py:40
  54.7 51.6 %copy-start.8 = (s32[256,32]{0,1:T(8,128)S(1)}, s32[256,32]{0,1:T(8,128)}, u32[]{:S(2)}) copy-start(s32[256,32]{0,1:T(8,128)} %param.12) | copy-start | bytes 98308
  54.7 51.6 %copy-start.9 = (s32[256,32]{0,1:T(8,128)S(1)}, s32[256,32]{0,1:T(8,128)}, u32[]{:S(2)}) copy-start(s32[256,32]{0,1:T(8,128)} %param.11) | copy-start | bytes 98308
  54.7 52.4 %copy-start.11 = (s32[2]{0:T(128)S(1)}, s32[2]{0:T(128)}, u32[]{:S(2)}) copy-start(s32[2]{0:T(128)} %constant.33) | copy-start | bytes 28
  54.7 52.5 %copy-start.12 = (s32[2]{0:T(128)S(1)}, s32[2]{0:T(128)}, u32[]{:S(2)}) copy-start(s32[2]{0:T(128)} %constant.36) | copy-start | bytes 28
  99.0 190.1 %all-to-all-start.1 = ((bf16[64,128,512]{2,1,0:T(8,128)(2,1)}), bf16[64,128,512]{2,1,0:T(8,128)(2,1)}, u32[]{:S(2)}, u32[]{:S(2)}) async-start(bf16[64,128,512]{2,1,0:T(8,128)(2,1)} %gather_fusion.2), calls=%async_computation.1 | async-start | bytes 16777216 | tf_op jit(solution)/shard_map/all_to_all | solution.py:41
  106.2 366.3 %reduce-scatter.4.cloned.1.call-start = ((), (), s32[]{:S(2)}) async-start(), calls=%async_computation.5 | async-start | bytes 2129920 | tf_op jit(solution)/shard_map/reduce_scatter | solution.py:81
  112.0 18.3 %copy-start.6 = (f32[256,512]{1,0:T(8,128)}, f32[256,512]{1,0:T(8,128)S(1)}, u32[]{:S(2)}) copy-start(f32[256,512]{1,0:T(8,128)S(1)} %get-tuple-element.17) | copy-start | bytes 1572868
  130.3 29.2 %copy-start.2 = (bf16[256,128]{1,0:T(8,128)(2,1)S(1)}, bf16[256,128]{1,0:T(8,128)(2,1)}, u32[]{:S(2)}) copy-start(bf16[256,128]{1,0:T(8,128)(2,1)} %param.7) | copy-start | bytes 196612
  130.3 56.6 %copy-start.10 = (s32[256]{0:T(256)S(1)}, s32[256]{0:T(256)}, u32[]{:S(2)}) copy-start(s32[256]{0:T(256)} %param.13) | copy-start | bytes 3076
  289.1 10.6 %copy-start.3 = (f32[256,8192]{1,0:T(8,128)S(1)}, f32[256,8192]{1,0:T(8,128)}, u32[]{:S(2)}) copy-start(f32[256,8192]{1,0:T(8,128)} %reshape.84) | copy-start | bytes 25165828
  299.8 22.3 %copy-start.5 = (bf16[8,256,128]{1,2,0:T(8,128)(2,1)S(1)}, bf16[8,256,128]{1,2,0:T(8,128)(2,1)}, u32[]{:S(2)}) copy-start(bf16[8,256,128]{1,2,0:T(8,128)(2,1)} %copy-done.4) | copy-start | bytes 1572868
  299.8 22.3 %copy-start.7 = (f32[256,512]{1,0:T(8,128)S(1)}, f32[256,512]{1,0:T(8,128)}, u32[]{:S(2)}) copy-start(f32[256,512]{1,0:T(8,128)} %copy-done.6) | copy-start | bytes 1572868
  324.7 331.7 %all-gather.6.cloned.1.call-start = ((), (), s32[]{:S(2)}) async-start(), calls=%async_computation.4 | async-start | bytes 1064960 | tf_op jit(solution)/shard_map/all_gather | solution.py:84
Sparse Core Ops, SparseCore 0:
  324.9 147.6 reduce-scatter.3
  576.8 79.5 all-gather.5
